TPU v7x, 32 devices: a whole 2x2x4 slice. The times are simulated.
32 devices in a mesh: orow: 8 (over z, x), ocol: 4 (over y, core).
Axes of the slice: x: 2, y: 2, z: 4, core: 2. Of those that a mesh axis runs over, the one named last changes fastest.
Arguments:
- integrals: bfloat16 [2304, 16, 384], P('ocol', 'orow'), may hold values from -0.29882812 to 0.29882812
- occ_count: int32 [8], replicated, may hold values from 1 to 2
- occ_energy: float32 [16], replicated, may hold values from -2 to -0.5
- vir_energy: float32 [384], replicated, may hold values from 0.3 to 2.5
- task_iblock: int32 [32, 1], replicated, may hold values from 0 to 7; in each aligned block of 32 rows (0 to 31, 32 to 63, ...) at most 8 rows name the same one
- task_jblock: int32 [32], replicated, may hold values from 0 to 7
Outputs:
- gamma_out: float32 [2304, 16, 384], P('ocol', 'orow')
- density: float32 [384, 384], replicated
Inputs may be any that keep to these rules, and one draw needn't show every extreme that they name: `task_iblock`: no first block is named by more than 8 tasks, and some first block by exactly 8.
All inputs are finite; a program needn't handle non-finite values.
Results may differ from a plain program's by a relative error of at most 0.0019.
Values may be sent and summed in bfloat16 or wider, within the bound.
A program may use at most 128 MiB of HBM per device.

v0:
```python
import jax
import jax.numpy as jnp
from jax import lax
from jax.sharding import PartitionSpec as P


def make_amplitudes(k_total, i_energy, j_energy, vir_energy, usable):
    slots = k_total.shape[0]
    orbitals = i_energy.shape[1]
    virtuals = vir_energy.shape[0]
    k_grid = k_total.reshape(slots, orbitals, virtuals, orbitals, virtuals)
    denominator = (
        i_energy[:, :, None, None, None]
        + j_energy[:, None, None, :, None]
        - vir_energy[None, None, :, None, None]
        - vir_energy[None, None, None, None, :]
    )
    values = (2.0 * k_grid - jnp.swapaxes(k_grid, 2, 4)) / denominator
    values = values * usable[:, None, None, None, None]
    return values.astype(jnp.bfloat16).reshape(slots, orbitals * virtuals, orbitals * virtuals)


def local(integrals, occ_count, occ_energy, vir_energy, task_iblock, task_jblock):
    aux_local = integrals.shape[0]
    orbitals = integrals.shape[1]
    virtuals = integrals.shape[2]
    span = orbitals * virtuals
    block_total = lax.axis_size("orow")
    col_total = lax.axis_size("ocol")
    my_row = lax.axis_index("orow")
    my_col = lax.axis_index("ocol")
    active = jnp.arange(orbitals) < occ_count[my_row]
    masked = integrals * active.astype(jnp.bfloat16)[None, :, None]
    gathered = lax.all_gather(masked, "orow", axis=1, tiled=True)
    flat_blocks = gathered.reshape(aux_local, block_total, span)
    first_list = task_iblock[:, 0]
    task_total = first_list.shape[0]
    per_row = task_total // block_total
    task_ids = my_row * per_row + jnp.arange(per_row)
    i_block = first_list[task_ids]
    j_block = task_jblock[task_ids]
    usable = jnp.ones((per_row,), jnp.float32)
    energy_grid = occ_energy.reshape(block_total, orbitals)
    i_rows = jnp.take(flat_blocks, i_block, axis=1)
    j_rows = jnp.take(flat_blocks, j_block, axis=1)
    k_partial = jnp.einsum("psx,psy->sxy", i_rows, j_rows, preferred_element_type=jnp.float32)
    slots = k_partial.shape[0]
    i_energy = energy_grid[i_block]
    j_energy = energy_grid[j_block]
    k_total = lax.psum(k_partial, "ocol")
    amplitudes = make_amplitudes(k_total, i_energy, j_energy, vir_energy, usable)
    gamma_i = jnp.einsum("sxy,psy->psx", amplitudes, j_rows, preferred_element_type=jnp.float32)
    gamma_j = jnp.einsum("sxy,psx->psy", amplitudes, i_rows, preferred_element_type=jnp.float32)
    slice_width = span // col_total
    amp_grid = amplitudes.reshape(slots, orbitals, virtuals, span)
    column_part = lax.dynamic_slice_in_dim(amp_grid, my_col * slice_width, slice_width, 3)
    dens_part = jnp.einsum(
        "siaw,sibw->ab", column_part, column_part, preferred_element_type=jnp.float32
    )
    block_ids = jnp.arange(block_total)
    i_onehot = (i_block[:, None] == block_ids[None, :]).astype(jnp.float32)
    j_onehot = (j_block[:, None] == block_ids[None, :]).astype(jnp.float32)
    buffer = jnp.einsum(
        "sk,psx->pkx", i_onehot, gamma_i, precision=lax.Precision.HIGHEST
    ) + jnp.einsum("sk,psx->pkx", j_onehot, gamma_j, precision=lax.Precision.HIGHEST)
    owned = lax.psum_scatter(buffer, "orow", scatter_dimension=1, tiled=True)
    gamma_out = owned.reshape(aux_local, orbitals, virtuals)
    density = lax.psum(dens_part, ("orow", "ocol")) / task_total
    return (gamma_out, density)


def solution(mesh):
    return jax.shard_map(
        local,
        mesh=mesh,
        in_specs=(P("ocol", "orow", None), P(), P(), P(), P(), P()),
        out_specs=(P("ocol", "orow", None), P()),
        check_vma=False,
    )
```

profile of v0, /device:TPU:0, one launch (start us, length us, event | category | flops | bytes accessed | tf_op | source)
XLA Modules:
  0.0 801.5 jit_solution(11271543090973514411)
XLA Ops:
  14.0 108.6 %all-gather.2.cloned.1.call-done = bf16[576,16,384]{2,0,1:T(8,128)(2,1)} async-done(((bf16[576,2,384]{2,0,1:T(8,128)(2,1)}), bf16[576,16,384]{2,0,1:T(8,128)(2,1)}) %all-gather.2.cloned.1.call-update) | async-done | bytes 7077904 | tf_op jit(solution)/shard_map/all_gather | solution.py:34
  122.6 10.1 %copy.40 = bf16[576,16,384]{2,1,0:T(8,128)(2,1)} copy(bf16[576,16,384]{2,0,1:T(8,128)(2,1)} %all-gather.2.cloned.1.call-done) | data formatting | bytes 14155776 | tf_op jit(solution)/shard_map/all_gather | solution.py:34
  132.7 11.3 %reshape.89 = bf16[576,8,768]{2,1,0:T(8,128)(2,1)} reshape(bf16[576,16,384]{2,1,0:T(8,128)(2,1)} %copy.40) | data formatting | bytes 14155776 | tf_op jit(solution)/shard_map/reshape | solution.py:35
  144.0 7.4 copy.41
  151.4 5.6 gather_fusion.5
  157.0 3.8 gather_fusion.4
  160.8 9.3 %fusion.7 = f32[4,768,768]{2,1,0:T(8,128)} fusion(bf16[4,576,768]{2,1,0:T(8,128)(2,1)S(1)} %gather_fusion.4, pred[4]{0:T(512)(128)(4,1)S(1)} %get-tuple-element.4, bf16[4,576,768]{2,1,0:T(8,128)(2,1)} %gather_fusion.5, pred[4]{0:T(512)(128)(4,1)S(1)} %copy-done.11), kind=kOutput, calls=%fused_computation.15 | convolution fusion | flops 2721447936 | bytes 16515080 | tf_op jit(solution)/shard_map/psx,psy->sxy/dot_general | solution.py:46
  170.1 12.5 %reshape.90 = f32[4,2,384,2,384]{4,3,2,1,0:T(2,128)} reshape(f32[4,768,768]{2,1,0:T(8,128)} %fusion.7) | data formatting | bytes 18874368 | tf_op jit(solution)/shard_map/reshape | solution.py:11
  182.6 14.8 %copy.43 = f32[4,2,384,2,384]{2,4,3,1,0:T(8,128)} copy(f32[4,2,384,2,384]{4,3,2,1,0:T(2,128)} %reshape.90) | data formatting | bytes 18874368 | tf_op jit(solution)/shard_map/reshape | solution.py:11
  201.4 164.2 %all-reduce.3.cloned.1.call-done = f32[4,2,384,2,384]{2,4,3,1,0:T(8,128)} async-done(((f32[4,2,384,2,384]{2,4,3,1,0:T(8,128)}), f32[4,2,384,2,384]{2,4,3,1,0:T(8,128)}) %all-reduce.3.cloned.1.call-update) | async-done | bytes 9437200 | tf_op jit(solution)/shard_map/psum | solution.py:50
  365.6 9.6 %copy.44 = f32[4,2,384,2,384]{4,2,3,1,0:T(8,128)} copy(f32[4,2,384,2,384]{2,4,3,1,0:T(8,128)} %all-reduce.3.cloned.1.call-done) | data formatting | bytes 18874368 | tf_op jit(solution)/shard_map/psum | solution.py:50
  375.2 9.6 %fusion.1 = bf16[4,2,384,2,384]{4,2,3,1,0:T(8,128)(2,1)} fusion(f32[4,2,384,2,384]{2,4,3,1,0:T(8,128)} %all-reduce.3.cloned.1.call-done, f32[4,2,384,2,384]{4,2,3,1,0:T(8,128)} %copy.44, f32[384]{0:T(512)S(1)} %copy-done.3, f32[4,2,384,2]{2,3,1,0:T(2,128)} %broadcast_subtract_fusion), kind=kLoop, calls=%fused_computation.9 | loop fusion | flops 11796480 | bytes 23619072 | tf_op jit(solution)/shard_map/convert_element_type | solution.py:20
  384.8 6.7 copy.52
  391.5 9.3 %copy.45 = bf16[4,2,384,2,384]{4,3,2,1,0:T(2,128)(2,1)} copy(bf16[4,2,384,2,384]{4,2,3,1,0:T(8,128)(2,1)} %fusion.1) | data formatting | bytes 9437184 | tf_op jit(solution)/shard_map/convert_element_type | solution.py:20
  400.8 11.3 %reshape.92 = bf16[4,768,768]{2,1,0:T(8,128)(2,1)} reshape(bf16[4,2,384,2,384]{4,3,2,1,0:T(2,128)(2,1)} %copy.45) | data formatting | bytes 9437184 | tf_op jit(solution)/shard_map/reshape | solution.py:20
  412.1 9.4 %fusion.15 = f32[576,4,768]{2,0,1:T(8,128)} fusion(bf16[4,768,768]{2,1,0:T(8,128)(2,1)} %reshape.92, bf16[4,576,768]{2,1,0:T(8,128)(2,1)} %gather_fusion.5, pred[4]{0:T(512)(128)(4,1)S(1)} %copy-done.12), kind=kOutput, calls=%fused_computation.23 | convolution fusion | flops 2719678464 | bytes 15335428 | tf_op jit(solution)/shard_map/sxy,psx->psy/dot_general | solution.py:53
  421.5 5.2 fusion.12
  426.8 3.3 convolution_bitcast_fusion
  430.1 14.4 %fusion.3 = f32[576,768,8]{1,2,0:T(8,128)S(1)} fusion(f32[576,4,768]{2,0,1:T(8,128)} %fusion.12, s32[4]{0:T(128)S(1)} %copy-done.5), kind=kOutput, calls=%fused_computation.11 | convolution fusion | flops 169869344 | bytes 21233680 | tf_op jit(solution)/shard_map/sk,psx->pkx/dot_general | solution.py:63
  444.6 18.4 %add_bitcast_fusion = f32[576,8,768]{2,1,0:T(8,128)} fusion(f32[576,768,8]{1,2,0:T(8,128)S(1)} %fusion.3, f32[576,4,768]{2,0,1:T(8,128)} %fusion.15, s32[4]{0:T(128)S(1)} %copy-done.7), kind=kOutput, calls=%fused_computation.6 | convolution fusion | flops 173408288 | bytes 35389456 | tf_op jit(solution)/shard_map/sk,psx->pkx/dot_general | solution.py:65
  462.9 14.7 %copy.48 = f32[576,8,768]{2,0,1:T(8,128)} copy(f32[576,8,768]{2,1,0:T(8,128)} %add_bitcast_fusion) | data formatting | bytes 28311552 | tf_op jit(solution)/shard_map/add | solution.py:63
  477.6 80.9 %all-reduce.5.cloned.1.call-done = f32[384,384]{1,0:T(8,128)} async-done(((f32[384,384]{1,0:T(8,128)}), f32[384,384]{1,0:T(8,128)}) %all-reduce.5.cloned.1.call-update) | async-done | bytes 589840 | tf_op jit(solution)/shard_map/psum | solution.py:68
  560.5 231.3 %reduce-scatter.2.cloned.1.call-done = f32[576,1,768]{2,0,1:T(8,128)} async-done(((f32[576,8,768]{2,0,1:T(8,128)}), f32[576,1,768]{2,0,1:T(8,128)}) %reduce-scatter.2.cloned.1.call-update) | async-done | bytes 1769488 | tf_op jit(solution)/shard_map/reduce_scatter | solution.py:66
  791.7 3.1 reshape.93
  (56 shorter events, 12.7 us)
Async XLA Ops:
  7.2 4.3 copy-start
  7.2 115.4 %all-gather.2.cloned.1.call-start = ((), (), s32[]{:S(2)}) async-start(), calls=%async_computation.1 | async-start | bytes 7962624 | tf_op jit(solution)/shard_map/all_gather | solution.py:34
  11.4 354.2 %all-reduce.3.cloned.1.call-start = ((), (), s32[]{:S(2)}) async-start(), calls=%async_computation.2 | async-start | bytes 18874368 | tf_op jit(solution)/shard_map/psum | solution.py:50
  12.1 120.6 %copy-start.4 = (s32[4]{0:T(128)}, s32[4]{0:T(128)S(1)}, u32[]{:S(2)}) copy-start(s32[4]{0:T(128)S(1)} %gather_fusion.1) | copy-start | bytes 52
  13.4 184.7 %copy-start.6 = (s32[4]{0:T(128)}, s32[4]{0:T(128)S(1)}, u32[]{:S(2)}) copy-start(s32[4]{0:T(128)S(1)} %gather_fusion) | copy-start | bytes 52
  14.0 146.8 %copy-start.9 = (pred[4]{0:T(512)(128)(4,1)}, pred[4]{0:T(512)(128)(4,1)S(1)}, u32[]{:S(2)}) copy-start(pred[4]{0:T(512)(128)(4,1)S(1)} %get-tuple-element.4) | copy-start | bytes 16
  157.0 3.8 copy-start.11
  197.4 0.7 copy-start.8
  197.4 3.3 copy-start.3
  197.4 361.1 %all-reduce.5.cloned.1.call-start = ((), (), s32[]{:S(2)}) async-start(), calls=%async_computation.4 | async-start | bytes 1179648 | tf_op jit(solution)/shard_map/psum | solution.py:68
  400.8 11.4 %copy-start.12 = (pred[4]{0:T(512)(128)(4,1)S(1)}, pred[4]{0:T(512)(128)(4,1)}, u32[]{:S(2)}) copy-start(pred[4]{0:T(512)(128)(4,1)} %get-tuple-element.3) | copy-start | bytes 16
  412.1 9.4 %copy-start.2 = (bf16[4,768,768]{2,1,0:T(8,128)(2,1)S(1)}, bf16[4,768,768]{2,1,0:T(8,128)(2,1)}, u32[]{:S(2)}) copy-start(bf16[4,768,768]{2,1,0:T(8,128)(2,1)} %reshape.92) | copy-start | bytes 14155780
  412.1 9.4 %copy-start.10 = (pred[4]{0:T(512)(128)(4,1)S(1)}, pred[4]{0:T(512)(128)(4,1)}, u32[]{:S(2)}) copy-start(pred[4]{0:T(512)(128)(4,1)} %copy-done.9) | copy-start | bytes 16
  421.5 8.6 %copy-start.5 = (s32[4]{0:T(128)S(1)}, s32[4]{0:T(128)}, u32[]{:S(2)}) copy-start(s32[4]{0:T(128)} %copy-done.4) | copy-start | bytes 52
  430.1 14.5 %copy-start.7 = (s32[4]{0:T(128)S(1)}, s32[4]{0:T(128)}, u32[]{:S(2)}) copy-start(s32[4]{0:T(128)} %copy-done.6) | copy-start | bytes 52
  430.1 361.6 %reduce-scatter.2.cloned.1.call-start = ((), (), s32[]{:S(2)}) async-start(), calls=%async_computation.3 | async-start | bytes 15925248 | tf_op jit(solution)/shard_map/reduce_scatter | solution.py:66
  477.6 317.1 %copy-start.1 = (s32[32,1]{0,1:T(1,128)S(1)}, s32[32,1]{0,1:T(1,128)}, u32[]{:S(2)}) copy-start(s32[32,1]{0,1:T(1,128)} %param.12) | copy-start | bytes 388
Sparse Core Ops, SparseCore 0:
  11.5 111.0 all-gather.1
  197.6 167.9 all-reduce.2
  430.2 128.3 all-reduce.4
  562.0 229.6 reduce-scatter.1
where the time goes:
time: 811 us; the launch traced here: 802 us
  waiting for transfers between devices  585 us (72%)
  local copies, waits for them, and re-layouts  125 us (15%)
  matrix products  60 us (7%)
  other arithmetic  16.9 us (2%)
  between operations  14.2 us (2%)
    reduce_scatter x1, waiting for transfers between devices, local(): owned = lax.psum_scatter(buffer, 'orow', scatter_dimension=1, tiled=True)  231 us
    psum x1, waiting for transfers between devices, local(): k_total = lax.psum(k_partial, 'ocol')  164 us
    all_gather x1, waiting for transfers between devices, local(): gathered = lax.all_gather(masked, 'orow', axis=1, tiled=True)  109 us
    psum x1, waiting for transfers between devices, local(): density = lax.psum(dens_part, ('orow', 'ocol')) / task_total  80.9 us
    reshape x2, local copies, waits for them, and re-layouts, make_amplitudes(): k_grid = k_total.reshape(slots, orbitals, virtuals, orbitals, virtuals)  27.3 us
    reshape x2, local copies, waits for them, and re-layouts, local(): flat_blocks = gathered.reshape(aux_local, block_total, span)  18.6 us
    dot_general x1, matrix products, local(): jnp.einsum('sk,psx->pkx', j_onehot, gamma_j, precision=lax.Precision.HIGH...  18.4 us
  transfers between devices with their start and end apart: 4, of which 4 were waited for; matrix products, arithmetic and copies ran while one was open for 7% of the time, Pallas kernels for 0%

commit v1 on v0

--- a/solution.py
+++ b/solution.py
@@ -47,7 +47,9 @@
     slots = k_partial.shape[0]
     i_energy = energy_grid[i_block]
     j_energy = energy_grid[j_block]
-    k_total = lax.psum(k_partial, "ocol")
+    k_total = k_partial
+    for hop in (1, 2):
+        k_total = k_total + lax.ppermute(k_total, "ocol", [(dev, dev ^ hop) for dev in range(4)])
     amplitudes = make_amplitudes(k_total, i_energy, j_energy, vir_energy, usable)
     gamma_i = jnp.einsum("sxy,psy->psx", amplitudes, j_rows, preferred_element_type=jnp.float32)
     gamma_j = jnp.einsum("sxy,psx->psy", amplitudes, i_rows, preferred_element_type=jnp.float32)

time: 811 us -> 873 us (1.076)
  waiting for transfers between devices: 585 us -> 636 us
  other arithmetic: 16.9 us -> 38.9 us
    ppermute x0 -> x2, waiting for transfers between devices: none -> 217 us  [local(): lax.ppermute(k_total, 'ocol', [(dev, dev ^ hop) for dev in range(4)])]
    psum x1 -> x0, waiting for transfers between devices: 164 us -> none  [local(): k_total = lax.psum(k_partial, 'ocol')]
    add x0 -> x2, other arithmetic: none -> 22.4 us  [local(): k_total + lax.ppermute(k_total, 'ocol', [(dev, dev ^ hop) for dev in rang...]
    psum x1 -> x0, local copies, waits for them, and re-layouts: 9.61 us -> none  [local(): k_total = lax.psum(k_partial, 'ocol')]
  transfers between devices with their start and end apart: 4 -> 5, of which waited for: 4 -> 5; matrix products, arithmetic and copies ran while one was open for 7% -> 6% of each run, Pallas kernels for 0% -> 0%
where the time goes in v1:
time: 873 us; the launch traced here: 867 us
  waiting for transfers between devices  636 us (73%)
  local copies, waits for them, and re-layouts  118 us (14%)
  matrix products  58.1 us (7%)
  other arithmetic  38.9 us (4%)
  between operations  14.2 us (2%)
    reduce_scatter x1, waiting for transfers between devices, local(): owned = lax.psum_scatter(buffer, 'orow', scatter_dimension=1, tiled=True)  231 us
    ppermute x2, waiting for transfers between devices, local(): lax.ppermute(k_total, 'ocol', [(dev, dev ^ hop) for dev in range(4)])  217 us
    all_gather x1, waiting for transfers between devices, local(): gathered = lax.all_gather(masked, 'orow', axis=1, tiled=True)  109 us
    psum x1, waiting for transfers between devices, local(): density = lax.psum(dens_part, ('orow', 'ocol')) / task_total  79 us
    reshape x2, local copies, waits for them, and re-layouts, make_amplitudes(): k_grid = k_total.reshape(slots, orbitals, virtuals, orbitals, virtuals)  29.9 us
    add x2, other arithmetic, local(): k_total + lax.ppermute(k_total, 'ocol', [(dev, dev ^ hop) for dev in rang...  22.4 us
    reshape x2, local copies, waits for them, and re-layouts, local(): flat_blocks = gathered.reshape(aux_local, block_total, span)  19.1 us
    dot_general x1, matrix products, local(): jnp.einsum('sk,psx->pkx', j_onehot, gamma_j, precision=lax.Precision.HIGH...  18.4 us
  transfers between devices with their start and end apart: 5, of which 5 were waited for; matrix products, arithmetic and copies ran while one was open for 6% of the time, Pallas kernels for 0%

profile of v1, /device:TPU:0, one launch (start us, length us, event | category | flops | bytes accessed | tf_op | source)
XLA Modules:
  0.0 867.0 jit_solution(5998633008376778003)
XLA Ops:
  14.1 108.5 %all-gather.2.cloned.1.call-done = bf16[576,16,384]{2,0,1:T(8,128)(2,1)} async-done(((bf16[576,2,384]{2,0,1:T(8,128)(2,1)}), bf16[576,16,384]{2,0,1:T(8,128)(2,1)}) %all-gather.2.cloned.1.call-update) | async-done | bytes 7077904 | tf_op jit(solution)/shard_map/all_gather | solution.py:34
  122.6 10.1 %copy.19 = bf16[576,16,384]{2,1,0:T(8,128)(2,1)} copy(bf16[576,16,384]{2,0,1:T(8,128)(2,1)} %all-gather.2.cloned.1.call-done) | data formatting | bytes 14155776 | tf_op jit(solution)/shard_map/all_gather | solution.py:34
  132.7 11.7 %reshape.89 = bf16[576,8,768]{2,1,0:T(8,128)(2,1)} reshape(bf16[576,16,384]{2,1,0:T(8,128)(2,1)} %copy.19) | data formatting | bytes 14155776 | tf_op jit(solution)/shard_map/reshape | solution.py:35
  144.4 7.4 copy.20
  151.8 5.6 gather_fusion.5
  157.4 3.8 gather_fusion.4
  161.2 7.6 fusion.7
  168.9 3.7 copy-done.2
  172.5 14.8 %collective-permute-done = f32[4,768,768]{2,1,0:T(8,128)} collective-permute-done((f32[4,768,768]{2,1,0:T(8,128)S(1)}, f32[4,768,768]{2,1,0:T(8,128)}, u32[]{:S(2)}, u32[]{:S(2)}) %collective-permute-start) | collective-permute-done | bytes 9437216 | tf_op jit(solution)/shard_map/ppermute | solution.py:52
  187.3 11.2 %add.91 = f32[4,768,768]{2,1,0:T(8,128)} add(f32[4,768,768]{2,1,0:T(8,128)} %copy-done.2, f32[4,768,768]{2,1,0:T(8,128)} %collective-permute-done) | non-fusion elementwise | flops 2359296 | bytes 28311552 | tf_op jit(solution)/shard_map/add | solution.py:52
  201.5 202.3 %collective-permute-done.1 = f32[4,768,768]{2,1,0:T(8,128)} collective-permute-done((f32[4,768,768]{2,1,0:T(8,128)}, f32[4,768,768]{2,1,0:T(8,128)}, u32[]{:S(2)}, u32[]{:S(2)}) %collective-permute-start.1) | collective-permute-done | bytes 9437216 | tf_op jit(solution)/shard_map/ppermute | solution.py:52
  403.8 11.2 %add.92 = f32[4,768,768]{2,1,0:T(8,128)} add(f32[4,768,768]{2,1,0:T(8,128)} %add.91, f32[4,768,768]{2,1,0:T(8,128)} %collective-permute-done.1) | non-fusion elementwise | flops 2359296 | bytes 28311552 | tf_op jit(solution)/shard_map/add | solution.py:52
  415.0 12.4 %reshape.90 = f32[4,2,384,2,384]{4,3,2,1,0:T(2,128)} reshape(f32[4,768,768]{2,1,0:T(8,128)} %add.92) | data formatting | bytes 18874368 | tf_op jit(solution)/shard_map/reshape | solution.py:11
  427.5 17.5 %copy.22 = f32[4,2,384,2,384]{2,3,4,1,0:T(2,128)} copy(f32[4,2,384,2,384]{4,3,2,1,0:T(2,128)} %reshape.90) | data formatting | bytes 18874368 | tf_op jit(solution)/shard_map/reshape | solution.py:11
  444.9 10.7 %fusion.1 = bf16[4,2,384,2,384]{4,3,2,1,0:T(2,128)(2,1)} fusion(f32[4,2,384,2,384]{2,3,4,1,0:T(2,128)} %copy.22, f32[4,2,384,2,384]{4,3,2,1,0:T(2,128)} %reshape.90, f32[384]{0:T(512)S(1)} %copy-done.5, f32[4,2,384,2]{3,2,1,0:T(8,128)S(1)} %broadcast_subtract_fusion), kind=kLoop, calls=%fused_computation.9 | loop fusion | flops 11796480 | bytes 23619072 | tf_op jit(solution)/shard_map/convert_element_type | solution.py:20
  455.6 11.5 %reshape.92 = bf16[4,768,768]{2,1,0:T(8,128)(2,1)} reshape(bf16[4,2,384,2,384]{4,3,2,1,0:T(2,128)(2,1)} %fusion.1) | data formatting | bytes 9437184 | tf_op jit(solution)/shard_map/reshape | solution.py:20
  467.2 12.4 %copy.26 = bf16[4,2,384,2,384]{2,4,3,0,1:T(8,128)(2,1)} copy(bf16[4,2,384,2,384]{4,3,2,1,0:T(2,128)(2,1)} %fusion.1) | data formatting | bytes 9437184 | tf_op jit(solution)/shard_map/convert_element_type | solution.py:20
  479.5 9.4 %fusion.15 = f32[576,4,768]{2,0,1:T(8,128)} fusion(bf16[4,768,768]{2,1,0:T(8,128)(2,1)} %reshape.92, bf16[4,576,768]{2,1,0:T(8,128)(2,1)} %gather_fusion.5, pred[4]{0:T(512)(128)(4,1)S(1)} %copy-done.9), kind=kOutput, calls=%fused_computation.23 | convolution fusion | flops 2719678464 | bytes 15335428 | tf_op jit(solution)/shard_map/sxy,psx->psy/dot_general | solution.py:55
  488.9 5.1 fusion.12
  497.4 14.4 %fusion.3 = f32[576,768,8]{1,2,0:T(8,128)S(1)} fusion(f32[576,4,768]{2,0,1:T(8,128)} %fusion.12, s32[4]{0:T(128)S(1)} %gather_fusion.1), kind=kOutput, calls=%fused_computation.11 | convolution fusion | flops 169869344 | bytes 21233680 | tf_op jit(solution)/shard_map/sk,psx->pkx/dot_general | solution.py:65
  511.8 18.4 %add_bitcast_fusion = f32[576,8,768]{2,1,0:T(8,128)} fusion(f32[576,768,8]{1,2,0:T(8,128)S(1)} %fusion.3, f32[576,4,768]{2,0,1:T(8,128)} %fusion.15, s32[4]{0:T(128)S(1)} %gather_fusion), kind=kOutput, calls=%fused_computation.6 | convolution fusion | flops 173408288 | bytes 35389456 | tf_op jit(solution)/shard_map/sk,psx->pkx/dot_general | solution.py:67
  530.2 14.6 %copy.25 = f32[576,8,768]{2,0,1:T(8,128)} copy(f32[576,8,768]{2,1,0:T(8,128)} %add_bitcast_fusion) | data formatting | bytes 28311552 | tf_op jit(solution)/shard_map/add | solution.py:65
  544.8 79.0 %all-reduce.2.cloned.1.call-done = f32[384,384]{1,0:T(8,128)} async-done(((f32[384,384]{1,0:T(8,128)}), f32[384,384]{1,0:T(8,128)}) %all-reduce.2.cloned.1.call-update) | async-done | bytes 589840 | tf_op jit(solution)/shard_map/psum | solution.py:70
  625.7 231.4 %reduce-scatter.2.cloned.1.call-done = f32[576,1,768]{2,0,1:T(8,128)} async-done(((f32[576,8,768]{2,0,1:T(8,128)}), f32[576,1,768]{2,0,1:T(8,128)}) %reduce-scatter.2.cloned.1.call-update) | async-done | bytes 1769488 | tf_op jit(solution)/shard_map/reduce_scatter | solution.py:68
  (56 shorter events, 18.1 us)
Async XLA Ops:
  7.2 4.3 copy-start
  7.2 115.4 %all-gather.2.cloned.1.call-start = ((), (), s32[]{:S(2)}) async-start(), calls=%async_computation.1 | async-start | bytes 7962624 | tf_op jit(solution)/shard_map/all_gather | solution.py:34
  11.4 612.4 %all-reduce.2.cloned.1.call-start = ((), (), s32[]{:S(2)}) async-start(), calls=%async_computation.3 | async-start | bytes 1179648 | tf_op jit(solution)/shard_map/psum | solution.py:70
  157.4 3.8 copy-start.7
  161.2 7.6 copy-start.3
  168.9 3.7 copy-start.2
  172.5 28.8 %copy-start.5 = (f32[384]{0:T(512)S(1)}, f32[384]{0:T(512)}, u32[]{:S(2)}) copy-start(f32[384]{0:T(512)} %param.11) | copy-start | bytes 4612
  172.5 14.8 %collective-permute-start = (f32[4,768,768]{2,1,0:T(8,128)S(1)}, f32[4,768,768]{2,1,0:T(8,128)}, u32[]{:S(2)}, u32[]{:S(2)}) collective-permute-start(f32[4,768,768]{2,1,0:T(8,128)S(1)} %fusion.7), channel_id=1, source_target_pairs={{0,1},{1,0},{2,3},{3,2},{4,5},{5,4},{6,7},{7,6},{8,9},{9,8},{10,11... | collective-permute-start | bytes 28311560 | tf_op jit(solution)/shard_map/ppermute | solution.py:52
  172.5 27.5 %copy-start.6 = (f32[16]{0:T(128)S(1)}, f32[16]{0:T(128)}, u32[]{:S(2)}) copy-start(f32[16]{0:T(128)} %param.10) | copy-start | bytes 196
  198.5 205.3 %collective-permute-start.1 = (f32[4,768,768]{2,1,0:T(8,128)}, f32[4,768,768]{2,1,0:T(8,128)}, u32[]{:S(2)}, u32[]{:S(2)}) collective-permute-start(f32[4,768,768]{2,1,0:T(8,128)} %add.91), channel_id=1, source_target_pairs={{0,2},{1,3},{2,0},{3,1},{4,6},{5,7},{6,4},{7,5},{8,10},{9,11},{10,... | collective-permute-start | bytes 28311560 | tf_op jit(solution)/shard_map/ppermute | solution.py:52
  467.2 12.4 %copy-start.9 = (pred[4]{0:T(512)(128)(4,1)S(1)}, pred[4]{0:T(512)(128)(4,1)}, u32[]{:S(2)}) copy-start(pred[4]{0:T(512)(128)(4,1)} %get-tuple-element.3) | copy-start | bytes 16
  467.2 21.8 %slice-start = ((s8[4718592]{0:T(1024)(128)(4,1)}), s8[524288]{0:T(1024)(128)(4,1)S(1)}, s32[]{:S(2)}) async-start(s8[4718592]{0:T(1024)(128)(4,1)} %bitcast.55), calls=%async_computation.4 | async-start | bytes 1048576
  479.5 9.4 %slice-start.1 = ((s8[4718592]{0:T(1024)(128)(4,1)}), s8[4194304]{0:T(1024)(128)(4,1)S(1)}, s32[]{:S(2)}) async-start(s8[4718592]{0:T(1024)(128)(4,1)} %bitcast.55), calls=%async_computation.5 | async-start | bytes 8388608
  479.5 9.4 %copy-start.4 = (bf16[4,576,768]{2,1,0:T(8,128)(2,1)S(1)}, bf16[4,576,768]{2,1,0:T(8,128)(2,1)}, u32[]{:S(2)}) copy-start(bf16[4,576,768]{2,1,0:T(8,128)(2,1)} %copy-done.3) | copy-start | bytes 10616836
  479.5 9.4 %copy-start.8 = (pred[4]{0:T(512)(128)(4,1)S(1)}, pred[4]{0:T(512)(128)(4,1)}, u32[]{:S(2)}) copy-start(pred[4]{0:T(512)(128)(4,1)} %get-tuple-element.4) | copy-start | bytes 16
  497.3 359.8 %reduce-scatter.2.cloned.1.call-start = ((), (), s32[]{:S(2)}) async-start(), calls=%async_computation.2 | async-start | bytes 15925248 | tf_op jit(solution)/shard_map/reduce_scatter | solution.py:68
  544.8 315.4 %copy-start.1 = (s32[32,1]{0,1:T(1,128)S(1)}, s32[32,1]{0,1:T(1,128)}, u32[]{:S(2)}) copy-start(s32[32,1]{0,1:T(1,128)} %param.12) | copy-start | bytes 388
Sparse Core Ops, SparseCore 0:
  11.5 111.0 all-gather.1
  497.4 126.3 all-reduce.1
  627.5 229.6 reduce-scatter.1
